TPU v7x, 32 devices: a whole 2x2x4 slice. The times are simulated.
32 devices in a mesh: dp: 4 (over z), seq: 8 (over y, x, core).
Axes of the slice: x: 2, y: 2, z: 4, core: 2. Of those that a mesh axis runs over, the one named last changes fastest.
Arguments:
- tokens: float32 [4, 1024, 2048], P('dp', 'seq'), may hold values from -10 to 10, as said below
- cotangent: float32 [4, 1024, 2048], P('dp', 'seq'), may hold values from -6 to 6
- short_weights: float32 [3, 8, 2048], replicated, may hold values from 0.2 to 0.6
Outputs:
- grad_tokens: float32 [4, 1024, 2048], P('dp', 'seq')
- grad_weights: float32 [3, 8, 2048], P(None, None, 'seq')
Inputs may be any that keep to these rules, and one draw needn't show every extreme that they name: `tokens`: Real-valued activations of order one.
All inputs are finite; a program needn't handle non-finite values.
Results may differ from a plain program's by a relative error of at most 0.0003.
Values sent between devices are 32-bit elements; how exact they have to be, the bound alone decides.
No kernel may reach another device: no remote copies, remote signals or barrier semaphores. Data moves between devices by JAX's collectives and lax.ppermute only.
A program may use at most 64 MiB of HBM per device.

v0:
```python
import jax
import jax.numpy as jnp
from jax import lax
from jax.sharding import PartitionSpec as P

HEAD = 64
D = 2048
K = 8


def attend_back(query, key, value, grad_o):
    scale = HEAD ** (-0.5)
    hi = lax.Precision.HIGHEST
    scores = scale * jnp.einsum("qhe,khe->hqk", query, key, precision=hi)
    top = jnp.max(scores, axis=-1, keepdims=True)
    expo = jnp.exp(scores - top)
    probs = expo / jnp.sum(expo, axis=-1, keepdims=True)
    grad_probs = jnp.einsum("qhe,khe->hqk", grad_o, value, precision=hi)
    delta = jnp.sum(probs * grad_probs, axis=-1, keepdims=True)
    grad_scores = probs * (grad_probs - delta)
    grad_q = scale * jnp.einsum("hqk,khe->qhe", grad_scores, key, precision=hi)
    grad_k = scale * jnp.einsum("hqk,qhe->khe", grad_scores, query, precision=hi)
    grad_v = jnp.einsum("hqk,qhe->khe", probs, grad_o, precision=hi)
    return (grad_q, grad_k, grad_v)


def head_backward(query, key, value, grad_o):
    batch, sums, width = query.shape
    heads_here = width // HEAD

    def one_sequence(parts):
        shaped = [p.reshape(sums, heads_here, HEAD) for p in parts]
        grads = attend_back(shaped[0], shaped[1], shaped[2], shaped[3])
        return tuple((g.reshape(sums, width) for g in grads))

    return jax.vmap(one_sequence)((query, key, value, grad_o))


def per_device(tokens, cotangent, short_weights):
    hi = lax.Precision.HIGHEST
    batch = tokens.shape[0]
    col_tokens, col_grad = (
        lax.all_to_all(tokens, "seq", split_axis=2, concat_axis=1, tiled=True),
        lax.all_to_all(cotangent, "seq", split_axis=2, concat_axis=1, tiled=True),
    )
    length = col_tokens.shape[1]
    width = col_tokens.shape[2]
    sums = length // K
    start = lax.axis_index("seq") * width
    local_weights = lax.dynamic_slice_in_dim(short_weights, start, width, 2)
    grouped = col_tokens.reshape(batch, sums, K, width)
    summary = jnp.einsum("bjic,mic->mbjc", grouped, local_weights, precision=hi)
    grad_o = jnp.sum(col_grad.reshape(batch, sums, K, width), axis=2)
    grad_q, grad_k, grad_v = head_backward(summary[0], summary[1], summary[2], grad_o)
    grad_summary = jnp.stack([grad_q, grad_k, grad_v])
    grad_cols = jnp.einsum("mbjc,mic->bjic", grad_summary, local_weights, precision=hi).reshape(
        batch, length, width
    )
    grad_tokens = lax.all_to_all(grad_cols, "seq", split_axis=1, concat_axis=2, tiled=True)
    partial_value = jnp.einsum("mbjc,bjic->mic", grad_summary, grouped, precision=hi)
    raw = lax.psum(partial_value, "dp")
    total_sq = lax.psum(jnp.sum(raw * raw), "seq")
    mean_sq = total_sq / (3 * K * D)
    factor = jnp.minimum(1.0, 1.0 / jnp.sqrt(mean_sq + 1e-06))
    return (grad_tokens, raw * factor)


def solution(mesh):
    return jax.shard_map(
        per_device,
        mesh=mesh,
        in_specs=(P("dp", "seq", None), P("dp", "seq", None), P()),
        out_specs=(P("dp", "seq", None), P(None, None, "seq")),
        check_vma=False,
    )
```

profile of v0, /device:TPU:0, one launch (start us, length us, event | category | flops | bytes accessed | tf_op | source)
XLA Modules:
  0.0 110.5 jit_solution(7120607152902859944)
XLA Ops:
  0.6 0.0 copy-start
  0.6 3.6 %copy.65 = f32[1,128,2048]{1,0,2:T(1,128)} copy(f32[1,128,2048]{2,1,0:T(8,128)} %param.4) | data formatting | bytes 2097152 | tf_op args[1]
  4.3 0.0 copy-start.1
  4.3 5.3 %all-to-all-start.1 = ((f32[1,128,2048]{1,0,2:T(1,128)}), f32[1,128,2048]{1,0,2:T(1,128)S(1)}, u32[]{:S(2)}, u32[]{:S(2)}) async-start(f32[1,128,2048]{1,0,2:T(1,128)} %copy.65), calls=%async_computation.1 | async-start | bytes 2097152 | tf_op jit(solution)/shard_map/all_to_all | solution.py:44
  9.6 0.0 copy-done.1
  9.6 1.9 %copy.62 = f32[1,128,2048]{1,0,2:T(1,128)} copy(f32[1,128,2048]{2,1,0:T(8,128)S(1)} %copy-done.1) | data formatting | bytes 2097152 | tf_op args[0]
  11.5 13.5 %all-to-all-done.1 = f32[1,128,2048]{1,0,2:T(1,128)S(1)} async-done(((f32[1,128,2048]{1,0,2:T(1,128)}), f32[1,128,2048]{1,0,2:T(1,128)S(1)}, u32[]{:S(2)}, u32[]{:S(2)}) %all-to-all-start.1) | async-done | bytes 1048608 | tf_op jit(solution)/shard_map/all_to_all | solution.py:44
  25.0 3.6 %all-to-all-start = ((f32[1,128,2048]{1,0,2:T(1,128)}), f32[1,128,2048]{1,0,2:T(1,128)S(1)}, u32[]{:S(2)}, u32[]{:S(2)}) async-start(f32[1,128,2048]{1,0,2:T(1,128)} %copy.62), calls=%async_computation | async-start | bytes 2097152 | tf_op jit(solution)/shard_map/all_to_all | solution.py:43
  28.6 0.0 copy-done
  28.6 0.2 copy.84
  28.8 1.3 %copy.66 = f32[1,8,128,256]{3,2,1,0:T(8,128)} copy(f32[1,8,128,256]{2,3,1,0:T(8,128)S(1)} %bitcast.64) | data formatting | bytes 2097152 | tf_op jit(solution)/shard_map/all_to_all | solution.py:44
  30.1 1.5 %reduce_sum.37 = f32[128,256]{1,0:T(8,128)S(1)} reduce(f32[128,8,256]{2,1,0:T(8,128)} %bitcast.65, f32[]{:T(128)} %constant.6.clone.1), dimensions={1}, to_apply=%region_2.0 | reduce | flops 229376 | bytes 1179652 | tf_op jit(solution)/shard_map/reduce_sum | solution.py:53
  31.6 0.1 copy.67
  31.7 12.2 %all-to-all-done = f32[1,128,2048]{1,0,2:T(1,128)S(1)} async-done(((f32[1,128,2048]{1,0,2:T(1,128)}), f32[1,128,2048]{1,0,2:T(1,128)S(1)}, u32[]{:S(2)}, u32[]{:S(2)}) %all-to-all-start) | async-done | bytes 1048608 | tf_op jit(solution)/shard_map/all_to_all | solution.py:43
  43.9 0.3 copy.63
  44.2 0.6 copy.64
  44.8 1.8 %convolution_bitcast_fusion.2 = f32[3,1,128,256]{2,0,3,1:T(4,128)S(1)} fusion(f32[3,8,256]{1,0,2:T(4,128)S(1)} %copy.84, f32[128,8,256]{0,1,2:T(8,128)S(1)} %copy.64), kind=kOutput, calls=%fused_computation.2 | convolution fusion | flops 9437184 | bytes 1466368 | tf_op jit(solution)/shard_map/bjic,mic->mbjc/dot_general | solution.py:52
  46.6 0.3 fusion.8
  46.8 0.6 fusion.9
  47.4 0.1 fusion.1
  47.5 0.6 fusion.5
  48.1 0.6 multiply_reduce_fusion.1
  48.7 0.6 convolution_multiply_fusion.1
  49.4 0.0 copy-start.2
  49.4 0.4 convolution_multiply_fusion.2
  49.8 0.0 copy-start.4
  49.8 0.2 copy-done.2
  50.0 0.4 copy-done.4
  50.4 3.4 %convolution_bitcast_fusion = f32[1,128,8,256]{1,2,3,0:T(8,128)} fusion(f32[3,8,256]{1,0,2:T(4,128)S(1)} %copy.84, f32[1,1,128,256]{2,0,3,1:T(1,128)S(1)} %bitcast.74, f32[1,1,128,256]{2,0,3,1:T(1,128)S(1)} %bitcast.76, f32[1,1,128,256]{2,0,3,1:T(1,128)S(1)} %bitcast.78), kind=kOutput, calls=%fused_computation | convolution fusion | flops 9633792 | bytes 1466368 | tf_op jit(solution)/shard_map/mbjc,mic->bjic/dot_general | solution.py:56
  53.8 1.7 %copy.74 = f32[1,128,8,256]{3,2,1,0:T(8,128)S(1)} copy(f32[1,128,8,256]{1,2,3,0:T(8,128)} %convolution_bitcast_fusion) | data formatting | bytes 2097152 | tf_op jit(solution)/shard_map/mbjc,mic->bjic/transpose | solution.py:56
  55.6 2.0 %copy.75 = f32[1,1024,256]{2,0,1:T(1,128)} copy(f32[1,1024,256]{2,1,0:T(8,128)S(1)} %bitcast.67) | data formatting | bytes 2097152 | tf_op jit(solution)/shard_map/reshape | solution.py:56
  57.6 0.0 copy-start.3
  57.6 0.0 copy-start.5
  57.6 3.9 %all-to-all-start.2 = ((f32[1,1024,256]{2,0,1:T(1,128)}), f32[1,1024,256]{2,0,1:T(1,128)S(1)}, u32[]{:S(2)}, u32[]{:S(2)}) async-start(f32[1,1024,256]{2,0,1:T(1,128)} %copy.75), calls=%async_computation.2 | async-start | bytes 2097152 | tf_op jit(solution)/shard_map/all_to_all | solution.py:59
  61.5 0.0 copy-done.3
  61.5 0.0 copy-done.5
  61.5 2.0 %convolution_bitcast_fusion.1 = f32[3,8,256]{1,0,2:T(4,128)S(1)} fusion(f32[128,8,256]{0,1,2:T(8,128)S(1)} %copy.64, f32[1,1,128,256]{2,0,3,1:T(1,128)S(1)} %bitcast.75, f32[1,1,128,256]{2,0,3,1:T(1,128)S(1)} %bitcast.77, f32[1,1,128,256]{2,0,3,1:T(1,128)S(1)} %bitcast.79), kind=kOutput, calls=%fused_computation.1 | convolution fusion | flops 9633792 | bytes 1466368 | tf_op jit(solution)/shard_map/mbjc,bjic->mic/dot_general | solution.py:60
  63.5 30.4 %psum.14 = f32[3,8,256]{1,0,2:T(4,128)S(1)} all-reduce(f32[3,8,256]{1,0,2:T(4,128)S(1)} %convolution_bitcast_fusion.1), channel_id=1, replica_groups=mesh['dp'=4,'seq'=8] {'dp'}, use_global_device_ids=true, to_apply=%region_4.0 | all-reduce | flops 6144 | bytes 49152 | tf_op jit(solution)/shard_map/psum | solution.py:61
  94.0 0.9 multiply_reduce_fusion
  94.8 12.4 %psum.15 = f32[]{:T(128)} all-reduce(f32[]{:T(128)} %multiply_reduce_fusion), channel_id=1, replica_groups=mesh['dp'=4,'seq'=8] {'seq'}, use_global_device_ids=true, to_apply=%region_6.0 | all-reduce | flops 1 | bytes 8 | tf_op jit(solution)/shard_map/psum | solution.py:62
  107.9 0.1 broadcast_multiply_fusion
  108.0 0.8 copy.79
  108.8 0.0 all-to-all-done.2
  108.8 0.1 copy.83
  108.9 0.3 copy.76
  109.2 1.3 %copy.78 = f32[1,128,2048]{2,1,0:T(8,128)} copy(f32[1,128,2048]{1,2,0:T(8,128)S(1)} %bitcast.69) | data formatting | bytes 2097152
  (1 shorter events, 0.0 us)
Async XLA Ops:
  0.6 27.9 %copy-start = (f32[3,8,2048]{2,1,0:T(8,128)S(1)}, f32[3,8,2048]{2,1,0:T(8,128)}, u32[]{:S(2)}) copy-start(f32[3,8,2048]{2,1,0:T(8,128)} %param.5) | copy-start | bytes 589828
  4.3 5.3 %copy-start.1 = (f32[1,128,2048]{2,1,0:T(8,128)S(1)}, f32[1,128,2048]{2,1,0:T(8,128)}, u32[]{:S(2)}) copy-start(f32[1,128,2048]{2,1,0:T(8,128)} %param.3) | copy-start | bytes 3145732
  4.3 20.7 %all-to-all-start.1 = ((f32[1,128,2048]{1,0,2:T(1,128)}), f32[1,128,2048]{1,0,2:T(1,128)S(1)}, u32[]{:S(2)}, u32[]{:S(2)}) async-start(f32[1,128,2048]{1,0,2:T(1,128)} %copy.65), calls=%async_computation.1 | async-start | bytes 2097152 | tf_op jit(solution)/shard_map/all_to_all | solution.py:44
  25.0 18.9 %all-to-all-start = ((f32[1,128,2048]{1,0,2:T(1,128)}), f32[1,128,2048]{1,0,2:T(1,128)S(1)}, u32[]{:S(2)}, u32[]{:S(2)}) async-start(f32[1,128,2048]{1,0,2:T(1,128)} %copy.62), calls=%async_computation | async-start | bytes 2097152 | tf_op jit(solution)/shard_map/all_to_all | solution.py:43
  49.4 0.6 copy-start.2
  49.8 0.7 copy-start.4
  57.6 3.9 %copy-start.3 = (f32[4,64,128]{2,1,0:T(8,128)S(1)}, f32[4,64,128]{2,1,0:T(8,128)}, u32[]{:S(2)}) copy-start(f32[4,64,128]{2,1,0:T(8,128)} %copy-done.2) | copy-start | bytes 393220
  57.6 3.9 %copy-start.5 = (f32[4,64,128]{2,1,0:T(8,128)S(1)}, f32[4,64,128]{2,1,0:T(8,128)}, u32[]{:S(2)}) copy-start(f32[4,64,128]{2,1,0:T(8,128)} %copy-done.4) | copy-start | bytes 393220
  57.6 51.2 %all-to-all-start.2 = ((f32[1,1024,256]{2,0,1:T(1,128)}), f32[1,1024,256]{2,0,1:T(1,128)S(1)}, u32[]{:S(2)}, u32[]{:S(2)}) async-start(f32[1,1024,256]{2,0,1:T(1,128)} %copy.75), calls=%async_computation.2 | async-start | bytes 2097152 | tf_op jit(solution)/shard_map/all_to_all | solution.py:59
where the time goes:
time: 111 us
  blocking collectives  42.8 us (39%)
  waiting for transfers between devices  25.6 us (23%)
  local copies, waits for them, and re-layouts  15.2 us (14%)
  starting transfers between devices  12.8 us (12%)
  matrix products  10 us (9%)
  other arithmetic  2.51 us (2%)
  between operations  1.53 us (1%)
    psum x1, blocking collectives, per_device(): raw = lax.psum(partial_value, 'dp')  30.4 us
    all_to_all x1, waiting for transfers between devices, per_device(): lax.all_to_all(cotangent, 'seq', split_axis=2, concat_axis=1, tiled=True)  13.5 us
    psum x1, blocking collectives, per_device(): total_sq = lax.psum(jnp.sum(raw * raw), 'seq')  12.4 us
    all_to_all x1, waiting for transfers between devices, per_device(): lax.all_to_all(tokens, 'seq', split_axis=2, concat_axis=1, tiled=True)  12.2 us
    unnamed x18, local copies, waits for them, and re-layouts  8.56 us
    all_to_all x1, starting transfers between devices, per_device(): lax.all_to_all(cotangent, 'seq', split_axis=2, concat_axis=1, tiled=True)  5.33 us
    all_to_all x1, starting transfers between devices, per_device(): lax.all_to_all(grad_cols, 'seq', split_axis=1, concat_axis=2, tiled=True)  3.87 us
    all_to_all x1, starting transfers between devices, per_device(): lax.all_to_all(tokens, 'seq', split_axis=2, concat_axis=1, tiled=True)  3.56 us
  transfers between devices with their start and end apart: 3, of which 2 were waited for; matrix products, arithmetic and copies ran while one was open for 8% of the time, Pallas kernels for 0%

commit v1 on v0

--- a/solution.py
+++ b/solution.py
@@ -2,6 +2,7 @@
 import jax.numpy as jnp
 from jax import lax
 from jax.sharding import PartitionSpec as P
+from jax.lax import all_gather
 
 HEAD = 64
 D = 2048
@@ -58,7 +59,7 @@
     )
     grad_tokens = lax.all_to_all(grad_cols, "seq", split_axis=1, concat_axis=2, tiled=True)
     partial_value = jnp.einsum("mbjc,bjic->mic", grad_summary, grouped, precision=hi)
-    raw = lax.psum(partial_value, "dp")
+    raw = all_gather(partial_value, "dp").sum(axis=0)
     total_sq = lax.psum(jnp.sum(raw * raw), "seq")
     mean_sq = total_sq / (3 * K * D)
     factor = jnp.minimum(1.0, 1.0 / jnp.sqrt(mean_sq + 1e-06))

time: 111 us -> 93 us (0.84)
  blocking collectives: 42.8 us -> 26 us
  local copies, waits for them, and re-layouts: 15.2 us -> 14 us
    psum x1 -> x0, blocking collectives: 30.4 us -> none  [per_device(): raw = lax.psum(partial_value, 'dp')]
    all_gather x0 -> x1, blocking collectives: none -> 13.6 us  [per_device(): raw = all_gather(partial_value, 'dp').sum(axis=0)]
    unnamed x18 -> x9, local copies, waits for them, and re-layouts: 8.56 us -> 7.15 us
  transfers between devices with their start and end apart: 3 -> 3, of which waited for: 2 -> 2; matrix products, arithmetic and copies ran while one was open for 8% -> 9% of each run, Pallas kernels for 0% -> 0%
where the time goes in v1:
time: 93 us; the launch traced here: 92.5 us
  blocking collectives  26 us (28%)
  waiting for transfers between devices  25.6 us (28%)
  local copies, waits for them, and re-layouts  14 us (15%)
  starting transfers between devices  12.6 us (14%)
  matrix products  10 us (11%)
  other arithmetic  2.77 us (3%)
  between operations  1.49 us (2%)
    all_gather x1, blocking collectives, per_device(): raw = all_gather(partial_value, 'dp').sum(axis=0)  13.6 us
    all_to_all x1, waiting for transfers between devices, per_device(): lax.all_to_all(cotangent, 'seq', split_axis=2, concat_axis=1, tiled=True)  13.5 us
    psum x1, blocking collectives, per_device(): total_sq = lax.psum(jnp.sum(raw * raw), 'seq')  12.4 us
    all_to_all x1, waiting for transfers between devices, per_device(): lax.all_to_all(tokens, 'seq', split_axis=2, concat_axis=1, tiled=True)  12.2 us
    unnamed x9, local copies, waits for them, and re-layouts  7.15 us
    all_to_all x1, starting transfers between devices, per_device(): lax.all_to_all(cotangent, 'seq', split_axis=2, concat_axis=1, tiled=True)  5.33 us
    all_to_all x1, starting transfers between devices, per_device(): lax.all_to_all(grad_cols, 'seq', split_axis=1, concat_axis=2, tiled=True)  3.74 us
    all_to_all x1, starting transfers between devices, per_device(): lax.all_to_all(tokens, 'seq', split_axis=2, concat_axis=1, tiled=True)  3.56 us
  transfers between devices with their start and end apart: 3, of which 2 were waited for; matrix products, arithmetic and copies ran while one was open for 9% of the time, Pallas kernels for 0%

profile of v1, /device:TPU:0, one launch (start us, length us, event | category | flops | bytes accessed | tf_op | source)
XLA Modules:
  0.0 92.5 jit_solution(5664738102535985116)
XLA Ops:
  0.6 0.0 copy-start
  0.6 3.6 %copy.64 = f32[1,128,2048]{1,0,2:T(1,128)} copy(f32[1,128,2048]{2,1,0:T(8,128)} %param.4) | data formatting | bytes 2097152 | tf_op args[1]
  4.3 0.0 copy-start.1
  4.3 5.3 %all-to-all-start.1 = ((f32[1,128,2048]{1,0,2:T(1,128)}), f32[1,128,2048]{1,0,2:T(1,128)S(1)}, u32[]{:S(2)}, u32[]{:S(2)}) async-start(f32[1,128,2048]{1,0,2:T(1,128)} %copy.64), calls=%async_computation.1 | async-start | bytes 2097152 | tf_op jit(solution)/shard_map/all_to_all | solution.py:45
  9.6 0.0 copy-done.1
  9.6 1.9 %copy.61 = f32[1,128,2048]{1,0,2:T(1,128)} copy(f32[1,128,2048]{2,1,0:T(8,128)S(1)} %copy-done.1) | data formatting | bytes 2097152 | tf_op args[0]
  11.5 13.5 %all-to-all-done.1 = f32[1,128,2048]{1,0,2:T(1,128)S(1)} async-done(((f32[1,128,2048]{1,0,2:T(1,128)}), f32[1,128,2048]{1,0,2:T(1,128)S(1)}, u32[]{:S(2)}, u32[]{:S(2)}) %all-to-all-start.1) | async-done | bytes 1048608 | tf_op jit(solution)/shard_map/all_to_all | solution.py:45
  25.0 3.6 %all-to-all-start = ((f32[1,128,2048]{1,0,2:T(1,128)}), f32[1,128,2048]{1,0,2:T(1,128)S(1)}, u32[]{:S(2)}, u32[]{:S(2)}) async-start(f32[1,128,2048]{1,0,2:T(1,128)} %copy.61), calls=%async_computation | async-start | bytes 2097152 | tf_op jit(solution)/shard_map/all_to_all | solution.py:44
  28.6 0.0 copy-done
  28.6 0.2 copy.83
  28.8 1.3 %copy.65 = f32[1,8,128,256]{3,2,1,0:T(8,128)} copy(f32[1,8,128,256]{2,3,1,0:T(8,128)S(1)} %bitcast.64) | data formatting | bytes 2097152 | tf_op jit(solution)/shard_map/all_to_all | solution.py:45
  30.1 1.5 %reduce_sum.46 = f32[128,256]{1,0:T(8,128)S(1)} reduce(f32[128,8,256]{2,1,0:T(8,128)} %bitcast.66, f32[]{:T(128)} %constant.6.clone.1), dimensions={1}, to_apply=%region_2.0 | reduce | flops 229376 | bytes 1179652 | tf_op jit(solution)/shard_map/reduce_sum | solution.py:54
  31.6 0.1 copy.66
  31.7 12.2 %all-to-all-done = f32[1,128,2048]{1,0,2:T(1,128)S(1)} async-done(((f32[1,128,2048]{1,0,2:T(1,128)}), f32[1,128,2048]{1,0,2:T(1,128)S(1)}, u32[]{:S(2)}, u32[]{:S(2)}) %all-to-all-start) | async-done | bytes 1048608 | tf_op jit(solution)/shard_map/all_to_all | solution.py:44
  43.9 0.3 copy.62
  44.2 0.6 copy.63
  44.8 1.8 %convolution_bitcast_fusion.2 = f32[3,1,128,256]{2,0,3,1:T(4,128)S(1)} fusion(f32[3,8,256]{1,0,2:T(4,128)S(1)} %copy.83, f32[128,8,256]{0,1,2:T(8,128)S(1)} %copy.63), kind=kOutput, calls=%fused_computation.2 | convolution fusion | flops 9437184 | bytes 1466368 | tf_op jit(solution)/shard_map/bjic,mic->mbjc/dot_general | solution.py:53
  46.6 0.3 fusion.8
  46.8 0.6 fusion.9
  47.4 0.1 fusion.1
  47.5 0.6 fusion.5
  48.1 0.6 multiply_reduce_fusion
  48.7 0.6 convolution_multiply_fusion.1
  49.4 0.4 convolution_multiply_fusion.2
  49.8 3.4 %convolution_bitcast_fusion = f32[1,128,8,256]{1,2,3,0:T(8,128)} fusion(f32[3,8,256]{1,0,2:T(4,128)S(1)} %copy.83, f32[1,1,128,256]{2,0,3,1:T(1,128)S(1)} %bitcast.75, f32[1,1,128,256]{2,0,3,1:T(1,128)S(1)} %bitcast.77, f32[1,1,128,256]{2,0,3,1:T(1,128)S(1)} %bitcast.79), kind=kOutput, calls=%fused_computation | convolution fusion | flops 9633792 | bytes 1466368 | tf_op jit(solution)/shard_map/mbjc,mic->bjic/dot_general | solution.py:57
  53.2 1.7 %copy.73 = f32[1,128,8,256]{3,2,1,0:T(8,128)S(1)} copy(f32[1,128,8,256]{1,2,3,0:T(8,128)} %convolution_bitcast_fusion) | data formatting | bytes 2097152 | tf_op jit(solution)/shard_map/mbjc,mic->bjic/transpose | solution.py:57
  54.9 2.0 %copy.74 = f32[1,1024,256]{2,0,1:T(1,128)} copy(f32[1,1024,256]{2,1,0:T(8,128)S(1)} %bitcast.68) | data formatting | bytes 2097152 | tf_op jit(solution)/shard_map/reshape | solution.py:57
  57.0 3.7 %all-to-all-start.2 = ((f32[1,1024,256]{2,0,1:T(1,128)}), f32[1,1024,256]{2,0,1:T(1,128)S(1)}, u32[]{:S(2)}, u32[]{:S(2)}) async-start(f32[1,1024,256]{2,0,1:T(1,128)} %copy.74), calls=%async_computation.2 | async-start | bytes 2097152 | tf_op jit(solution)/shard_map/all_to_all | solution.py:60
  60.7 2.0 %convolution_bitcast_fusion.1 = f32[3,8,256]{1,0,2:T(4,128)S(1)} fusion(f32[128,8,256]{0,1,2:T(8,128)S(1)} %copy.63, f32[1,1,128,256]{2,0,3,1:T(1,128)S(1)} %bitcast.76, f32[1,1,128,256]{2,0,3,1:T(1,128)S(1)} %bitcast.78, f32[1,1,128,256]{2,0,3,1:T(1,128)S(1)} %bitcast.80), kind=kOutput, calls=%fused_computation.1 | convolution fusion | flops 9633792 | bytes 1466368 | tf_op jit(solution)/shard_map/mbjc,bjic->mic/dot_general | solution.py:61
  62.7 0.1 copy.77
  62.9 13.6 %all-gather = f32[12,8,256]{2,1,0:T(8,128)S(1)} all-gather(f32[3,8,256]{2,1,0:T(8,128)S(1)} %copy.77), channel_id=2, replica_groups=mesh['dp'=4,'seq'=8] {'dp'}, dimensions={0}, use_global_device_ids=true | all-gather | bytes 122880 | tf_op jit(solution)/shard_map/all_gather | solution.py:62
  76.5 0.6 multiply_reduce_fusion.1
  77.1 12.4 %psum.7 = f32[]{:T(128)} all-reduce(f32[]{:T(128)} %multiply_reduce_fusion.1), channel_id=1, replica_groups=mesh['dp'=4,'seq'=8] {'seq'}, use_global_device_ids=true, to_apply=%region_6.0 | all-reduce | flops 1 | bytes 8 | tf_op jit(solution)/shard_map/psum | solution.py:63
  90.2 0.6 broadcast_multiply_fusion
  90.8 0.0 all-to-all-done.2
  90.8 0.1 copy.82
  90.9 0.3 copy.75
  91.2 1.3 %copy.78 = f32[1,128,2048]{2,1,0:T(8,128)} copy(f32[1,128,2048]{1,2,0:T(8,128)S(1)} %bitcast.70) | data formatting | bytes 2097152
  (2 shorter events, 0.0 us)
Async XLA Ops:
  0.6 27.9 %copy-start = (f32[3,8,2048]{2,1,0:T(8,128)S(1)}, f32[3,8,2048]{2,1,0:T(8,128)}, u32[]{:S(2)}) copy-start(f32[3,8,2048]{2,1,0:T(8,128)} %param.5) | copy-start | bytes 589828
  4.3 5.3 %copy-start.1 = (f32[1,128,2048]{2,1,0:T(8,128)S(1)}, f32[1,128,2048]{2,1,0:T(8,128)}, u32[]{:S(2)}) copy-start(f32[1,128,2048]{2,1,0:T(8,128)} %param.3) | copy-start | bytes 3145732
  4.3 20.7 %all-to-all-start.1 = ((f32[1,128,2048]{1,0,2:T(1,128)}), f32[1,128,2048]{1,0,2:T(1,128)S(1)}, u32[]{:S(2)}, u32[]{:S(2)}) async-start(f32[1,128,2048]{1,0,2:T(1,128)} %copy.64), calls=%async_computation.1 | async-start | bytes 2097152 | tf_op jit(solution)/shard_map/all_to_all | solution.py:45
  25.0 18.9 %all-to-all-start = ((f32[1,128,2048]{1,0,2:T(1,128)}), f32[1,128,2048]{1,0,2:T(1,128)S(1)}, u32[]{:S(2)}, u32[]{:S(2)}) async-start(f32[1,128,2048]{1,0,2:T(1,128)} %copy.61), calls=%async_computation | async-start | bytes 2097152 | tf_op jit(solution)/shard_map/all_to_all | solution.py:44
  57.0 33.8 %all-to-all-start.2 = ((f32[1,1024,256]{2,0,1:T(1,128)}), f32[1,1024,256]{2,0,1:T(1,128)S(1)}, u32[]{:S(2)}, u32[]{:S(2)}) async-start(f32[1,1024,256]{2,0,1:T(1,128)} %copy.74), calls=%async_computation.2 | async-start | bytes 2097152 | tf_op jit(solution)/shard_map/all_to_all | solution.py:60
